TPU v7x, 32 devices: a whole 2x2x4 slice. The times are simulated.
32 devices in a mesh: ha: 2 (over y), wa: 4 (over z), hd: 4 (over x, core).
Axes of the slice: x: 2, y: 2, z: 4, core: 2. Of those that a mesh axis runs over, the one named last changes fastest.
Arguments:
- q_raw: bfloat16 [2, 4, 128, 2560], P('ha', 'wa', None, 'hd')
- k_raw: bfloat16 [2, 4, 128, 2560], P('ha', 'wa', None, 'hd')
- values: bfloat16 [2, 4, 128, 2560], P('ha', 'wa', None, 'hd')
- upstream: bfloat16 [2, 4, 128, 2560], P('ha', 'wa', None, 'hd'), may hold values from -384 to 384
- outputs: bfloat16 [2, 4, 128, 2560], P('ha', 'wa', None, 'hd')
- logsumexp: float32 [2, 4, 20, 128], P('ha', 'wa', 'hd'), may hold values from 7.5 to 9.5
- gain_q: bfloat16 [2560], P('hd'), may hold values from 0.25 to 1.75
- gain_k: bfloat16 [2560], P('hd'), may hold values from 0.25 to 1.75
- far_list: int32 [2, 4, 12], P('ha'), may hold values from -1 to 15, as said below
Outputs:
- dq_raw: bfloat16 [2, 4, 128, 2560], P('ha', 'wa', None, 'hd')
- dk_raw: bfloat16 [2, 4, 128, 2560], P('ha', 'wa', None, 'hd')
- dv: bfloat16 [2, 4, 128, 2560], P('ha', 'wa', None, 'hd')
Inputs may be any that keep to these rules, and one draw needn't show every extreme that they name: far_list[r, c, f] is -1 (an empty slot) or names key unit u of tile (r, u // 4); the named tiles lie two or more columns away from c, and each is named at most once in far_list[r, c].
All inputs are finite; a program needn't handle non-finite values.
Results may differ from a plain program's by a relative error of at most 0.0015.
The roundings to bfloat16 on the way count: a program that leaves them out, or rounds other values in their place, can miss the bound.
Values may be sent and summed in bfloat16 or wider, within the bound.
A program may use at most 64 MiB of HBM per device.

v0:
```python
import math

import jax
import jax.numpy as jnp
from jax import lax
from jax.sharding import PartitionSpec as P

HEADS = 20
HEAD = 128
UNITS = 4


EPS = 1e-06
POSITIONS = ((1, 1), (0, 1), (2, 1), (1, 0), (1, 2))
CONTRACT_LAST = (((1,), (1,)), ((), ()))
CONTRACT_FIRST = (((0,), (0,)), ((), ()))


def with_halo(cells, sides, width):
    for axis, dim in sides:
        count = lax.axis_size(axis)
        ends = count - 1
        head = lax.slice_in_dim(cells, 0, width, axis=dim)
        tail = lax.slice_in_dim(cells, cells.shape[dim] - width, cells.shape[dim], axis=dim)
        cells = jnp.concatenate(
            [
                lax.ppermute(tail, axis, [(i, (i + 1) % count) for i in range(ends)]),
                cells,
                lax.ppermute(head, axis, [((i + 1) % count, i) for i in range(ends)]),
            ],
            axis=dim,
        )
    return cells


def shifted(value, axis, steps):
    count = lax.axis_size(axis)
    first, last = (max(0, -steps), min(count, count - steps))
    return lax.ppermute(value, axis, [(source, source + steps) for source in range(first, last)])


def tile_grads(queries, upstream_tile, lse_tile, delta_tile, keys, vals, key_valid):
    heads = lse_tile.shape[0]
    head_width = queries.shape[1] // heads
    score_scale = 1.0 / math.sqrt(head_width)
    query_parts = []
    key_parts = []
    value_parts = []
    for head_index in range(heads):
        lower = head_index * head_width
        upper = lower + head_width
        query_head = queries[:, lower:upper]
        upstream_head = upstream_tile[:, lower:upper]
        key_head = keys[:, lower:upper]
        value_head = vals[:, lower:upper]
        scores = (
            lax.dot_general(query_head, key_head, CONTRACT_LAST, preferred_element_type=jnp.float32)
            * score_scale
        )
        weight = jnp.where(key_valid[None, :], jnp.exp(scores - lse_tile[head_index][:, None]), 0.0)
        dweight = lax.dot_general(
            upstream_head, value_head, CONTRACT_LAST, preferred_element_type=jnp.float32
        )
        dscore = (weight * (dweight - delta_tile[head_index][:, None])).astype(jnp.bfloat16)
        query_parts.append(
            jnp.dot(dscore, key_head, preferred_element_type=jnp.float32) * score_scale
        )
        key_parts.append(
            lax.dot_general(dscore, query_head, CONTRACT_FIRST, preferred_element_type=jnp.float32)
            * score_scale
        )
        value_parts.append(
            lax.dot_general(
                weight.astype(jnp.bfloat16),
                upstream_head,
                CONTRACT_FIRST,
                preferred_element_type=jnp.float32,
            )
        )
    query_grad = jnp.concatenate(query_parts, axis=1)
    key_grad = jnp.concatenate(key_parts, axis=1).astype(jnp.bfloat16)
    value_grad = jnp.concatenate(value_parts, axis=1).astype(jnp.bfloat16)
    return (query_grad, key_grad, value_grad)


def body(q_raw, k_raw, values, upstream, outputs, logsumexp, gain_q, gain_k, far_list):
    row_index = lax.axis_index("ha")
    col_index = lax.axis_index("wa")
    rows_total = lax.axis_size("ha")
    cols_total = lax.axis_size("wa")
    query_raw = q_raw[0, 0]
    key_raw = k_raw[0, 0]
    value_tile = values[0, 0]
    upstream_tile = upstream[0, 0]
    output_tile = outputs[0, 0]
    lse_tile = logsumexp[0, 0]
    heads = lse_tile.shape[0]
    tokens = query_raw.shape[0]
    width = query_raw.shape[1]
    head_width = width // heads
    full_width = HEADS * HEAD
    gain_qw = gain_q.astype(jnp.float32)
    gain_kw = gain_k.astype(jnp.float32)
    query_wide = query_raw.astype(jnp.float32)
    key_wide = key_raw.astype(jnp.float32)
    squares = lax.psum(
        (jnp.sum(query_wide * query_wide, axis=1), jnp.sum(key_wide * key_wide, axis=1)), "hd"
    )
    q_rate = lax.rsqrt(squares[0] / full_width + EPS)
    k_rate = lax.rsqrt(squares[1] / full_width + EPS)
    query_norm = (query_wide * q_rate[:, None] * gain_qw).astype(jnp.bfloat16)
    key_norm = (key_wide * k_rate[:, None] * gain_kw).astype(jnp.bfloat16)
    product = upstream_tile.astype(jnp.float32) * output_tile.astype(jnp.float32)
    delta = jnp.sum(product.reshape(tokens, heads, head_width), axis=2).T
    exists = jnp.stack(
        [
            (row_index + row_step - 1 >= 0)
            & (row_index + row_step - 1 < rows_total)
            & (col_index + col_step - 1 >= 0)
            & (col_index + col_step - 1 < cols_total)
            for row_step, col_step in POSITIONS
        ]
    )
    win_valid = jnp.repeat(exists, tokens)
    window_len = 5 * tokens
    lists = far_list[0]
    owner_of = jnp.where(lists >= 0, lists // UNITS, -1)
    mine_owner = lax.dynamic_index_in_dim(owner_of, col_index, 0, keepdims=False)
    peer_ids = jnp.arange(cols_total, dtype=jnp.int32)
    slot_used = jnp.any(mine_owner[None, :] == peer_ids[:, None], axis=1)
    asked = owner_of == col_index
    send_unit = jnp.sum(jnp.where(asked, lists % UNITS, 0), axis=1)
    send_used = jnp.any(asked, axis=1)
    key_block = tokens // UNITS
    far_len = cols_total * key_block
    pair_local = jnp.stack([key_norm, value_tile])
    packed = jnp.take(pair_local.reshape(2, UNITS, key_block, width), send_unit, axis=1)
    far_pair = lax.all_to_all(packed, "wa", split_axis=1, concat_axis=1, tiled=True)
    far_keys = far_pair[0].reshape(far_len, width)
    far_vals = far_pair[1].reshape(far_len, width)
    far_valid = jnp.repeat(slot_used, key_block)
    grid = with_halo(pair_local[None, None], (("ha", 0), ("wa", 1)), 1)
    win_pairs = jnp.stack([grid[row_step, col_step, :2] for row_step, col_step in POSITIONS])
    win_keys = win_pairs[:, 0].reshape(window_len, width)
    win_vals = win_pairs[:, 1].reshape(window_len, width)
    all_keys = jnp.concatenate([win_keys, far_keys], axis=0)
    all_vals = jnp.concatenate([win_vals, far_vals], axis=0)
    all_valid = jnp.concatenate([win_valid, far_valid], axis=0)
    dq_wide, all_dk, all_dv = tile_grads(
        query_norm, upstream_tile, lse_tile, delta, all_keys, all_vals, all_valid
    )
    far_dk = all_dk[all_dk.shape[0] - far_len :]
    far_dv = all_dv[all_dv.shape[0] - far_len :]
    win_dk = all_dk[:window_len]
    win_dv = all_dv[:window_len]
    dq_norm = dq_wide.astype(jnp.bfloat16)
    far_parts = jnp.stack([far_dk, far_dv]).reshape(2, cols_total, key_block, width)
    returned = lax.all_to_all(far_parts, "wa", split_axis=1, concat_axis=1, tiled=True)
    picker = (
        (send_unit[:, None] == jnp.arange(UNITS, dtype=jnp.int32)[None, :]) & send_used[:, None]
    ).astype(jnp.bfloat16)
    total = jnp.einsum(
        "su,xskw->xukw", picker, returned, preferred_element_type=jnp.float32
    ).reshape(2, tokens, width)
    parts = jnp.stack([win_dk, win_dv]).reshape(2, 5, tokens, width)
    total = total + parts[:, 0].astype(jnp.float32)
    for position, step in ((1, -1), (2, 1)):
        total = total + shifted(parts[:, position], "ha", step).astype(jnp.float32)
    for position, step in ((3, -1), (4, 1)):
        total = total + shifted(parts[:, position], "wa", step).astype(jnp.float32)
    dk_norm = total[0].astype(jnp.bfloat16)
    dv_tile = total[1].astype(jnp.bfloat16)
    dq_float = dq_norm.astype(jnp.float32)
    dk_float = dk_norm.astype(jnp.float32)
    dots = lax.psum(
        (
            jnp.sum(gain_qw * dq_float * query_wide, axis=1),
            jnp.sum(gain_kw * dk_float * key_wide, axis=1),
        ),
        "hd",
    )
    dq_tile = (
        q_rate[:, None] * gain_qw * dq_float
        - query_wide * (q_rate**3 * dots[0] / full_width)[:, None]
    ).astype(jnp.bfloat16)
    dk_tile = (
        k_rate[:, None] * gain_kw * dk_float
        - key_wide * (k_rate**3 * dots[1] / full_width)[:, None]
    ).astype(jnp.bfloat16)
    return (dq_tile[None, None], dk_tile[None, None], dv_tile[None, None])


def solution(mesh):
    return jax.shard_map(
        body,
        mesh=mesh,
        in_specs=(
            P("ha", "wa", None, "hd"),
            P("ha", "wa", None, "hd"),
            P("ha", "wa", None, "hd"),
            P("ha", "wa", None, "hd"),
            P("ha", "wa", None, "hd"),
            P("ha", "wa", "hd", None),
            P("hd"),
            P("hd"),
            P("ha", None, None),
        ),
        out_specs=(P("ha", "wa", None, "hd"), P("ha", "wa", None, "hd"), P("ha", "wa", None, "hd")),
        check_vma=False,
    )
```

profile of v0, /device:TPU:0, one launch (start us, length us, event | category | flops | bytes accessed | tf_op | source)
XLA Modules:
  0.0 103.8 jit_solution(9262242221224043072)
XLA Ops:
  0.7 1.1 %copy.59 = bf16[1,1,128,640]{2,3,1,0:T(8,128)(2,1)S(1)} copy(bf16[1,1,128,640]{3,2,1,0:T(8,128)(2,1)} %param.9) | data formatting | bytes 327680 | tf_op args[0]
  1.9 1.0 fusion.80
  3.6 8.3 %all-reduce.1 = (f32[128]{0:T(128)S(1)}, f32[128]{0:T(128)S(1)}) all-reduce(f32[128]{0:T(128)S(1)} %fusion.57, f32[128]{0:T(128)S(1)} %fusion.80), channel_id=1, replica_groups=mesh['ha'=2,'wa'=4,'hd'=4] {'hd'}, use_global_device_ids=true, to_apply=%region_1.0 | all-reduce | flops 256 | bytes 2048 | tf_op jit(solution)/shard_map/psum | solution.py:106
  12.0 1.0 fusion.82
  13.0 1.0 fusion.84
  14.0 3.6 %collective-permute-start = (bf16[1,1,2,128,640]{4,3,2,1,0:T(8,128)(2,1)S(1)}, bf16[1,1,2,128,640]{4,3,2,1,0:T(8,128)(2,1)S(1)}, u32[]{:S(2)}, u32[]{:S(2)}) collective-permute-start(bf16[1,1,2,128,640]{4,3,2,1,0:T(8,128)(2,1)S(1)} %fusion.84), channel_id=1, source_target_pairs={{0,16},{1,17},{2,18},{3,19},{4,20},{5,21},{6,22},{7,23},{8,24},{9,... | collective-permute-start | bytes 983048 | tf_op jit(solution)/shard_map/ppermute | solution.py:27
  17.6 1.3 %collective-permute-start.1 = (bf16[1,1,2,128,640]{4,3,2,1,0:T(8,128)(2,1)S(1)}, bf16[1,1,2,128,640]{4,3,2,1,0:T(8,128)(2,1)S(1)}, u32[]{:S(2)}, u32[]{:S(2)}) collective-permute-start(bf16[1,1,2,128,640]{4,3,2,1,0:T(8,128)(2,1)S(1)} %fusion.84), channel_id=1, source_target_pairs={{16,0},{17,1},{18,2},{19,3},{20,4},{21,5},{22,6},{23,7},{24,8},{25... | collective-permute-start | bytes 983048 | tf_op jit(solution)/shard_map/ppermute | solution.py:29
  20.6 0.8 select_bitcast_fusion
  21.4 4.9 %all-to-all-start = ((bf16[2,4,32,640]{3,2,0,1:T(8,128)(2,1)}), bf16[2,4,32,640]{3,2,0,1:T(8,128)(2,1)S(1)}, u32[]{:S(2)}, u32[]{:S(2)}) async-start(bf16[2,4,32,640]{3,2,0,1:T(8,128)(2,1)} %select_bitcast_fusion), calls=%async_computation | async-start | bytes 655360 | tf_op jit(solution)/shard_map/all_to_all | solution.py:138
  27.0 0.8 fusion.59
  27.8 1.1 %pad_maximum_fusion = bf16[3,1,2,128,640]{4,3,2,1,0:T(8,128)(2,1)} fusion(bf16[1,1,2,128,640]{4,3,2,1,0:T(8,128)(2,1)S(1)} %collective-permute-done.1, bf16[1,1,2,128,640]{4,3,2,1,0:T(8,128)(2,1)S(1)} %fusion.84, bf16[1,1,2,128,640]{4,3,2,1,0:T(8,128)(2,1)S(1)} %collective-permute-done), kind=kLoop, calls=%fused_computation.93 | loop fusion | flops 983040 | bytes 1966080 | tf_op jit(solution)/shard_map/concatenate | solution.py:25
  28.9 4.9 %collective-permute-start.2 = (bf16[3,1,2,128,640]{4,3,2,1,0:T(8,128)(2,1)}, bf16[3,1,2,128,640]{4,3,2,1,0:T(8,128)(2,1)}, u32[]{:S(2)}, u32[]{:S(2)}) collective-permute-start(bf16[3,1,2,128,640]{4,3,2,1,0:T(8,128)(2,1)} %pad_maximum_fusion), channel_id=1, source_target_pairs={{0,4},{4,8},{8,12},{1,5},{5,9},{9,13},{2,6},{6,10},{10,14},{3,7},{... | collective-permute-start | bytes 2949128 | tf_op jit(solution)/shard_map/ppermute | solution.py:27
  34.1 1.3 %collective-permute-start.3 = (bf16[3,1,2,128,640]{4,3,2,1,0:T(8,128)(2,1)}, bf16[3,1,2,128,640]{4,3,2,1,0:T(8,128)(2,1)}, u32[]{:S(2)}, u32[]{:S(2)}) collective-permute-start(bf16[3,1,2,128,640]{4,3,2,1,0:T(8,128)(2,1)} %pad_maximum_fusion), channel_id=1, source_target_pairs={{4,0},{8,4},{12,8},{5,1},{9,5},{13,9},{6,2},{10,6},{14,10},{7,3},{... | collective-permute-start | bytes 2949128 | tf_op jit(solution)/shard_map/ppermute | solution.py:29
  35.6 16.5 %collective-permute-done.2 = bf16[3,1,2,128,640]{4,3,2,1,0:T(8,128)(2,1)} collective-permute-done((bf16[3,1,2,128,640]{4,3,2,1,0:T(8,128)(2,1)}, bf16[3,1,2,128,640]{4,3,2,1,0:T(8,128)(2,1)}, u32[]{:S(2)}, u32[]{:S(2)}) %collective-permute-start.2) | collective-permute-done | bytes 983072 | tf_op jit(solution)/shard_map/ppermute | solution.py:27
  52.1 1.0 fusion.79
  53.1 4.4 %collective-permute-done.3 = bf16[3,1,2,128,640]{4,3,2,1,0:T(8,128)(2,1)} collective-permute-done((bf16[3,1,2,128,640]{4,3,2,1,0:T(8,128)(2,1)}, bf16[3,1,2,128,640]{4,3,2,1,0:T(8,128)(2,1)}, u32[]{:S(2)}, u32[]{:S(2)}) %collective-permute-start.3) | collective-permute-done | bytes 983072 | tf_op jit(solution)/shard_map/ppermute | solution.py:29
  57.5 1.0 fusion.78
  64.9 0.9 constant_dynamic-update-slice_fusion.2
  65.8 0.9 constant_dynamic-update-slice_fusion.1
  68.5 3.5 %all-to-all-start.1 = ((bf16[2,4,32,640]{3,2,0,1:T(8,128)(2,1)}), bf16[2,4,32,640]{3,2,0,1:T(8,128)(2,1)S(1)}, u32[]{:S(2)}, u32[]{:S(2)}) async-start(bf16[2,4,32,640]{3,2,0,1:T(8,128)(2,1)} %copy.69), calls=%async_computation.1 | async-start | bytes 655360 | tf_op jit(solution)/shard_map/all_to_all | solution.py:158
  72.0 0.9 copy.72
  72.9 0.9 copy.73
  73.9 1.0 fusion.74
  74.9 3.9 %collective-permute-start.7 = (bf16[2,128,640]{2,1,0:T(8,128)(2,1)}, bf16[2,128,640]{2,1,0:T(8,128)(2,1)S(1)}, u32[]{:S(2)}, u32[]{:S(2)}) collective-permute-start(bf16[2,128,640]{2,1,0:T(8,128)(2,1)} %get-tuple-element.24), channel_id=1, source_target_pairs={{0,4},{4,8},{8,12},{1,5},{5,9},{9,13},{2,6},{6,10},{10,14},{3,7},{... | collective-permute-start | bytes 983048 | tf_op jit(solution)/shard_map/ppermute | solution.py:39
  78.8 1.3 %collective-permute-start.6 = (bf16[2,128,640]{2,1,0:T(8,128)(2,1)}, bf16[2,128,640]{2,1,0:T(8,128)(2,1)}, u32[]{:S(2)}, u32[]{:S(2)}) collective-permute-start(bf16[2,128,640]{2,1,0:T(8,128)(2,1)} %get-tuple-element.25), channel_id=1, source_target_pairs={{4,0},{8,4},{12,8},{5,1},{9,5},{13,9},{6,2},{10,6},{14,10},{7,3},{... | collective-permute-start | bytes 983048 | tf_op jit(solution)/shard_map/ppermute | solution.py:39
  80.1 5.0 %collective-permute-start.5 = (bf16[2,128,640]{2,1,0:T(8,128)(2,1)}, bf16[2,128,640]{2,1,0:T(8,128)(2,1)}, u32[]{:S(2)}, u32[]{:S(2)}) collective-permute-start(bf16[2,128,640]{2,1,0:T(8,128)(2,1)} %get-tuple-element.23), channel_id=1, source_target_pairs={{0,16},{1,17},{2,18},{3,19},{4,20},{5,21},{6,22},{7,23},{8,24},{9,... | collective-permute-start | bytes 983048 | tf_op jit(solution)/shard_map/ppermute | solution.py:39
  85.1 1.3 %collective-permute-start.4 = (bf16[2,128,640]{2,1,0:T(8,128)(2,1)S(1)}, bf16[2,128,640]{2,1,0:T(8,128)(2,1)}, u32[]{:S(2)}, u32[]{:S(2)}) collective-permute-start(bf16[2,128,640]{2,1,0:T(8,128)(2,1)S(1)} %get-tuple-element.22), channel_id=1, source_target_pairs={{16,0},{17,1},{18,2},{19,3},{20,4},{21,5},{22,6},{23,7},{24,8},{25... | collective-permute-start | bytes 983048 | tf_op jit(solution)/shard_map/ppermute | solution.py:39
  86.9 0.9 convolution_bitcast_fusion
  88.1 1.2 %collective-permute-done.5 = bf16[2,128,640]{2,1,0:T(8,128)(2,1)} collective-permute-done((bf16[2,128,640]{2,1,0:T(8,128)(2,1)}, bf16[2,128,640]{2,1,0:T(8,128)(2,1)}, u32[]{:S(2)}, u32[]{:S(2)}) %collective-permute-start.5) | collective-permute-done | bytes 327712 | tf_op jit(solution)/shard_map/ppermute | solution.py:39
  89.3 4.9 %collective-permute-done.4 = bf16[2,128,640]{2,1,0:T(8,128)(2,1)} collective-permute-done((bf16[2,128,640]{2,1,0:T(8,128)(2,1)S(1)}, bf16[2,128,640]{2,1,0:T(8,128)(2,1)}, u32[]{:S(2)}, u32[]{:S(2)}) %collective-permute-start.4) | collective-permute-done | bytes 327712 | tf_op jit(solution)/shard_map/ppermute | solution.py:39
  94.2 1.4 %fusion.53 = bf16[2,128,640]{2,1,0:T(8,128)(2,1)S(1)} fusion(f32[2,4,32,640]{3,2,1,0:T(8,128)S(1)} %copy.71, bf16[2,128,640]{2,1,0:T(8,128)(2,1)S(1)} %collective-permute-done.7, bf16[2,128,640]{2,1,0:T(8,128)(2,1)} %collective-permute-done.6, bf16[2,128,640]{2,1,0:T(8,128)(2,1)} %collective-permute-done.5, bf16[2,128,640]{2,1,0:T(8,128)(2,1)} %collective-permute-done.4, ...), kind=kLoop, calls=%fused_computation.106 | loop fusion | flops 2457600 | bytes 3932160 | tf_op jit(solution)/shard_map/add | solution.py:170
  96.4 5.6 %all-reduce = (f32[128]{0:T(128)S(1)}, f32[128]{0:T(128)S(1)}) all-reduce(f32[128]{0:T(128)S(1)} %fusion.60, f32[128]{0:T(128)S(1)} %fusion.68), channel_id=1, replica_groups=mesh['ha'=2,'wa'=4,'hd'=4] {'hd'}, use_global_device_ids=true, to_apply=%region_8.9 | all-reduce | flops 256 | bytes 2048 | tf_op jit(solution)/shard_map/psum | solution.py:175
  (121 shorter events, 14.8 us)
Async XLA Ops:
  0.6 19.2 %copy-start = (bf16[1,1,128,640]{3,2,1,0:T(8,128)(2,1)S(1)}, bf16[1,1,128,640]{3,2,1,0:T(8,128)(2,1)}, u32[]{:S(2)}) copy-start(bf16[1,1,128,640]{3,2,1,0:T(8,128)(2,1)} %param.10) | copy-start | bytes 491524
  0.6 19.3 %copy-start.1 = (bf16[1,1,128,640]{3,2,1,0:T(8,128)(2,1)S(1)}, bf16[1,1,128,640]{3,2,1,0:T(8,128)(2,1)}, u32[]{:S(2)}) copy-start(bf16[1,1,128,640]{3,2,1,0:T(8,128)(2,1)} %param.11) | copy-start | bytes 491524
  0.7 18.3 %copy-start.10 = (s32[1,4,12]{2,1,0:T(4,128)S(1)}, s32[1,4,12]{2,1,0:T(4,128)}, u32[]{:S(2)}) copy-start(s32[1,4,12]{2,1,0:T(4,128)} %param.17) | copy-start | bytes 580
  12.0 1.0 %copy-start.17 = (f32[128]{0:T(128)}, f32[128]{0:T(128)S(1)}, u32[]{:S(2)}) copy-start(f32[128]{0:T(128)S(1)} %get-tuple-element.18) | copy-start | bytes 1540
  12.0 14.6 %copy-start.15 = (f32[128]{0:T(128)}, f32[128]{0:T(128)S(1)}, u32[]{:S(2)}) copy-start(f32[128]{0:T(128)S(1)} %get-tuple-element.17) | copy-start | bytes 1540
  14.0 12.3 %copy-start.11 = (f32[1,1,5,128]{3,1,2,0:T(1,128)S(1)}, f32[1,1,5,128]{3,1,2,0:T(1,128)}, u32[]{:S(2)}) copy-start(f32[1,1,5,128]{3,1,2,0:T(1,128)} %param.14) | copy-start | bytes 7684
  14.0 12.5 %copy-start.12 = (bf16[640]{0:T(1024)(128)(2,1)S(1)}, bf16[640]{0:T(1024)(128)(2,1)}, u32[]{:S(2)}) copy-start(bf16[640]{0:T(1024)(128)(2,1)} %param.15) | copy-start | bytes 3844
  14.0 12.5 %copy-start.7 = (bf16[1,1,128,640]{3,2,1,0:T(8,128)(2,1)S(1)}, bf16[1,1,128,640]{3,2,1,0:T(8,128)(2,1)}, u32[]{:S(2)}) copy-start(bf16[1,1,128,640]{3,2,1,0:T(8,128)(2,1)} %param.13) | copy-start | bytes 491524
  14.0 13.8 %collective-permute-start = (bf16[1,1,2,128,640]{4,3,2,1,0:T(8,128)(2,1)S(1)}, bf16[1,1,2,128,640]{4,3,2,1,0:T(8,128)(2,1)S(1)}, u32[]{:S(2)}, u32[]{:S(2)}) collective-permute-start(bf16[1,1,2,128,640]{4,3,2,1,0:T(8,128)(2,1)S(1)} %fusion.84), channel_id=1, source_target_pairs={{0,16},{1,17},{2,18},{3,19},{4,20},{5,21},{6,22},{7,23},{8,24},{9,... | collective-permute-start | bytes 983048 | tf_op jit(solution)/shard_map/ppermute | solution.py:27
  17.6 10.2 %collective-permute-start.1 = (bf16[1,1,2,128,640]{4,3,2,1,0:T(8,128)(2,1)S(1)}, bf16[1,1,2,128,640]{4,3,2,1,0:T(8,128)(2,1)S(1)}, u32[]{:S(2)}, u32[]{:S(2)}) collective-permute-start(bf16[1,1,2,128,640]{4,3,2,1,0:T(8,128)(2,1)S(1)} %fusion.84), channel_id=1, source_target_pairs={{16,0},{17,1},{18,2},{19,3},{20,4},{21,5},{22,6},{23,7},{24,8},{25... | collective-permute-start | bytes 983048 | tf_op jit(solution)/shard_map/ppermute | solution.py:29
  19.8 6.9 %copy-start.2 = (bf16[1,1,128,640]{3,2,1,0:T(8,128)(2,1)S(1)}, bf16[1,1,128,640]{3,2,1,0:T(8,128)(2,1)}, u32[]{:S(2)}) copy-start(bf16[1,1,128,640]{3,2,1,0:T(8,128)(2,1)} %param.12) | copy-start | bytes 491524
  21.4 14.1 %all-to-all-start = ((bf16[2,4,32,640]{3,2,0,1:T(8,128)(2,1)}), bf16[2,4,32,640]{3,2,0,1:T(8,128)(2,1)S(1)}, u32[]{:S(2)}, u32[]{:S(2)}) async-start(bf16[2,4,32,640]{3,2,0,1:T(8,128)(2,1)} %select_bitcast_fusion), calls=%async_computation | async-start | bytes 655360 | tf_op jit(solution)/shard_map/all_to_all | solution.py:138
  26.5 2.4 %copy-start.13 = (f32[128]{0:T(128)}, f32[128]{0:T(128)S(1)}, u32[]{:S(2)}) copy-start(f32[128]{0:T(128)S(1)} %add_rsqrt_fusion.1) | copy-start | bytes 1540
  28.9 23.2 %collective-permute-start.2 = (bf16[3,1,2,128,640]{4,3,2,1,0:T(8,128)(2,1)}, bf16[3,1,2,128,640]{4,3,2,1,0:T(8,128)(2,1)}, u32[]{:S(2)}, u32[]{:S(2)}) collective-permute-start(bf16[3,1,2,128,640]{4,3,2,1,0:T(8,128)(2,1)} %pad_maximum_fusion), channel_id=1, source_target_pairs={{0,4},{4,8},{8,12},{1,5},{5,9},{9,13},{2,6},{6,10},{10,14},{3,7},{... | collective-permute-start | bytes 2949128 | tf_op jit(solution)/shard_map/ppermute | solution.py:27
  34.1 23.4 %collective-permute-start.3 = (bf16[3,1,2,128,640]{4,3,2,1,0:T(8,128)(2,1)}, bf16[3,1,2,128,640]{4,3,2,1,0:T(8,128)(2,1)}, u32[]{:S(2)}, u32[]{:S(2)}) collective-permute-start(bf16[3,1,2,128,640]{4,3,2,1,0:T(8,128)(2,1)} %pad_maximum_fusion), channel_id=1, source_target_pairs={{4,0},{8,4},{12,8},{5,1},{9,5},{13,9},{6,2},{10,6},{14,10},{7,3},{... | collective-permute-start | bytes 2949128 | tf_op jit(solution)/shard_map/ppermute | solution.py:29
  58.5 0.9 copy-start.3
  66.7 1.8 %copy-start.4 = (bf16[1,1,128,640]{2,3,1,0:T(8,128)(2,1)}, bf16[1,1,128,640]{2,3,1,0:T(8,128)(2,1)S(1)}, u32[]{:S(2)}) copy-start(bf16[1,1,128,640]{2,3,1,0:T(8,128)(2,1)S(1)} %get-tuple-element.46) | copy-start | bytes 491524
  68.5 18.4 %all-to-all-start.1 = ((bf16[2,4,32,640]{3,2,0,1:T(8,128)(2,1)}), bf16[2,4,32,640]{3,2,0,1:T(8,128)(2,1)S(1)}, u32[]{:S(2)}, u32[]{:S(2)}) async-start(bf16[2,4,32,640]{3,2,0,1:T(8,128)(2,1)} %copy.69), calls=%async_computation.1 | async-start | bytes 655360 | tf_op jit(solution)/shard_map/all_to_all | solution.py:158
  73.9 12.5 %copy-start.6 = (bf16[128,640]{0,1:T(8,128)(2,1)S(1)}, bf16[128,640]{0,1:T(8,128)(2,1)}, u32[]{:S(2)}) copy-start(bf16[128,640]{0,1:T(8,128)(2,1)} %constant_dynamic-update-slice_fusion.9) | copy-start | bytes 491524
  73.9 12.5 %copy-start.8 = (bf16[128,128]{0,1:T(8,128)(2,1)S(1)}, bf16[128,128]{0,1:T(8,128)(2,1)}, u32[]{:S(2)}) copy-start(bf16[128,128]{0,1:T(8,128)(2,1)} %get-tuple-element.45) | copy-start | bytes 98308
  73.9 12.5 %copy-start.9 = (bf16[128,128]{0,1:T(8,128)(2,1)S(1)}, bf16[128,128]{0,1:T(8,128)(2,1)}, u32[]{:S(2)}) copy-start(bf16[128,128]{0,1:T(8,128)(2,1)} %get-tuple-element.47) | copy-start | bytes 98308
  73.9 12.6 %copy-start.5 = (bf16[1,1,128,640]{2,3,1,0:T(8,128)(2,1)S(1)}, bf16[1,1,128,640]{2,3,1,0:T(8,128)(2,1)}, u32[]{:S(2)}) copy-start(bf16[1,1,128,640]{2,3,1,0:T(8,128)(2,1)} %copy-done.4) | copy-start | bytes 491524
  74.9 13.1 %collective-permute-start.7 = (bf16[2,128,640]{2,1,0:T(8,128)(2,1)}, bf16[2,128,640]{2,1,0:T(8,128)(2,1)S(1)}, u32[]{:S(2)}, u32[]{:S(2)}) collective-permute-start(bf16[2,128,640]{2,1,0:T(8,128)(2,1)} %get-tuple-element.24), channel_id=1, source_target_pairs={{0,4},{4,8},{8,12},{1,5},{5,9},{9,13},{2,6},{6,10},{10,14},{3,7},{... | collective-permute-start | bytes 983048 | tf_op jit(solution)/shard_map/ppermute | solution.py:39
  78.8 9.3 %collective-permute-start.6 = (bf16[2,128,640]{2,1,0:T(8,128)(2,1)}, bf16[2,128,640]{2,1,0:T(8,128)(2,1)}, u32[]{:S(2)}, u32[]{:S(2)}) collective-permute-start(bf16[2,128,640]{2,1,0:T(8,128)(2,1)} %get-tuple-element.25), channel_id=1, source_target_pairs={{4,0},{8,4},{12,8},{5,1},{9,5},{13,9},{6,2},{10,6},{14,10},{7,3},{... | collective-permute-start | bytes 983048 | tf_op jit(solution)/shard_map/ppermute | solution.py:39
  80.1 9.2 %collective-permute-start.5 = (bf16[2,128,640]{2,1,0:T(8,128)(2,1)}, bf16[2,128,640]{2,1,0:T(8,128)(2,1)}, u32[]{:S(2)}, u32[]{:S(2)}) collective-permute-start(bf16[2,128,640]{2,1,0:T(8,128)(2,1)} %get-tuple-element.23), channel_id=1, source_target_pairs={{0,16},{1,17},{2,18},{3,19},{4,20},{5,21},{6,22},{7,23},{8,24},{9,... | collective-permute-start | bytes 983048 | tf_op jit(solution)/shard_map/ppermute | solution.py:39
  85.1 9.1 %collective-permute-start.4 = (bf16[2,128,640]{2,1,0:T(8,128)(2,1)S(1)}, bf16[2,128,640]{2,1,0:T(8,128)(2,1)}, u32[]{:S(2)}, u32[]{:S(2)}) collective-permute-start(bf16[2,128,640]{2,1,0:T(8,128)(2,1)S(1)} %get-tuple-element.22), channel_id=1, source_target_pairs={{16,0},{17,1},{18,2},{19,3},{20,4},{21,5},{22,6},{23,7},{24,8},{25... | collective-permute-start | bytes 983048 | tf_op jit(solution)/shard_map/ppermute | solution.py:39
  88.0 14.1 %copy-start.16 = (f32[128]{0:T(128)S(1)}, f32[128]{0:T(128)}, u32[]{:S(2)}) copy-start(f32[128]{0:T(128)} %copy-done.15) | copy-start | bytes 1540
  88.0 14.1 %copy-start.18 = (f32[128]{0:T(128)S(1)}, f32[128]{0:T(128)}, u32[]{:S(2)}) copy-start(f32[128]{0:T(128)} %copy-done.17) | copy-start | bytes 1540
  88.0 14.1 %copy-start.14 = (f32[128]{0:T(128)S(1)}, f32[128]{0:T(128)}, u32[]{:S(2)}) copy-start(f32[128]{0:T(128)} %copy-done.13) | copy-start | bytes 1540
where the time goes:
time: 105 us; the launch traced here: 104 us
  starting transfers between devices  30.8 us (29%)
  waiting for transfers between devices  27.1 us (26%)
  blocking collectives  14 us (13%)
  other arithmetic  11.4 us (11%)
  local copies, waits for them, and re-layouts  11 us (10%)
  matrix products  8.17 us (8%)
  between operations  1.39 us (1%)
    ppermute x2, waiting for transfers between devices, with_halo(): lax.ppermute(tail, axis, [(i, (i + 1) % count) for i in range(ends)])  16.5 us
    ppermute x4, starting transfers between devices, shifted(): lax.ppermute(value, axis, [(source, source + steps) for source in range(f...  11.5 us
    ppermute x2, starting transfers between devices, with_halo(): lax.ppermute(tail, axis, [(i, (i + 1) % count) for i in range(ends)])  8.44 us
    psum x1, blocking collectives, body(): lax.psum((jnp.sum(query_wide * query_wide, axis=1), jnp.sum(key_wide * ke...  8.34 us
    ppermute x4, waiting for transfers between devices, shifted(): lax.ppermute(value, axis, [(source, source + steps) for source in range(f...  6.17 us
    psum x1, blocking collectives, body(): lax.psum((jnp.sum(gain_qw * dq_float * query_wide, axis=1), jnp.sum(gain_...  5.63 us
    unnamed x49, local copies, waits for them, and re-layouts  4.89 us
    all_to_all x1, starting transfers between devices, body(): lax.all_to_all(packed, 'wa', split_axis=1, concat_axis=1, tiled=True)  4.87 us
  transfers between devices with their start and end apart: 10, of which 5 were waited for; matrix products, arithmetic and copies ran while one was open for 10% of the time, Pallas kernels for 0%

commit v1 on v0

v1 whole, which is shorter than its diff:
```python
import functools
import math

import jax
import jax.numpy as jnp
from jax import lax
from jax.experimental import pallas as pl
from jax.experimental.pallas import tpu as pltpu
from jax.sharding import PartitionSpec as P

UNITS = 4
EPS = 1e-06
MESH = pl.DeviceIdType.MESH
LAST = (((1,), (1,)), ((), ()))
FIRST = (((0,), (0,)), ((), ()))
PLAIN = (((1,), (0,)), ((), ()))
UP, DOWN, LEFT, RIGHT = range(4)
F32 = jnp.float32
BF16 = jnp.bfloat16


def dot(a, b, dims):
    return lax.dot_general(a, b, dims, preferred_element_type=F32)


def kernel(
    sizes,
    q_hbm,
    k_hbm,
    v_hbm,
    u_hbm,
    o_hbm,
    lse_ref,
    gain_q_ref,
    gain_k_ref,
    far_ref,
    dq_out,
    dk_out,
    dv_out,
    q_raw,
    k_raw,
    vals,
    ups,
    outs,
    qn,
    kn,
    delta_ref,
    dq_acc,
    own,
    halo,
    far_pack,
    far_in,
    ret_out,
    ret_in,
    fret_out,
    fret_in,
    total,
    xbuf,
    load_sem,
    halo_send,
    halo_recv,
    far_send,
    far_recv,
    ret_send,
    ret_recv,
    fret_send,
    fret_recv,
    x_send,
    x_recv,
):
    rows, cols, parts = sizes
    row = lax.axis_index("ha")
    col = lax.axis_index("wa")
    me = lax.axis_index("hd")
    tokens, width = q_raw.shape
    heads = lse_ref.shape[2]
    hw = width // heads
    kb = tokens // UNITS
    full_width = width * parts
    slots = far_ref.shape[2]
    score_scale = 1.0 / math.sqrt(hw)

    loads = []
    for index, (source, target) in enumerate(
        ((k_hbm, k_raw), (q_hbm, q_raw), (v_hbm, vals), (u_hbm, ups), (o_hbm, outs))
    ):
        copy = pltpu.make_async_copy(source.at[0, 0], target, load_sem.at[index])
        copy.start()
        loads.append(copy)

    exists = (row > 0, row < rows - 1, col > 0, col < cols - 1)
    ids = ({"ha": row - 1}, {"ha": row + 1}, {"wa": col - 1}, {"wa": col + 1})
    is_far = [(col - peer) * (col - peer) >= 4 for peer in range(cols)]

    barrier = pltpu.get_barrier_semaphore()
    hd_ids = [{"hd": lax.rem(me + off, parts)} for off in range(1, parts)]
    for target in hd_ids:
        pl.semaphore_signal(barrier, inc=1, device_id=target, device_id_type=MESH)
    for side in range(4):

        @pl.when(exists[side])
        def _(side=side):
            pl.semaphore_signal(barrier, inc=1, device_id=ids[side], device_id_type=MESH)

    for peer in range(cols):

        @pl.when(is_far[peer])
        def _(peer=peer):
            pl.semaphore_signal(barrier, inc=1, device_id={"wa": peer}, device_id_type=MESH)

    def lane_columns(columns):
        lane = lax.broadcasted_iota(jnp.int32, (tokens, 128), 1)
        mat = jnp.zeros((tokens, 128), F32)
        for place, column in columns:
            mat = jnp.where(lane == place, column, mat)
        return mat.T

    def row_sums(block):
        acc = block[:, :hw]
        for head in range(1, heads):
            acc = acc + block[:, head * hw : (head + 1) * hw]
        return jnp.sum(acc, axis=1, keepdims=True)

    def to_columns(rows8):
        return jnp.concatenate([rows8] * (tokens // 8), axis=0).T

    def x_copy(which, off):
        return pltpu.make_async_remote_copy(
            src_ref=xbuf.at[which, me],
            dst_ref=xbuf.at[which, me],
            send_sem=x_send.at[which, off],
            recv_sem=x_recv.at[which, off],
            device_id=hd_ids[off - 1],
            device_id_type=MESH,
        )

    def x_start(which, rows8):
        xbuf[which, me] = rows8
        for off in range(1, parts):
            x_copy(which, off).start()

    def x_finish(which):
        for off in range(1, parts):
            x_copy(which, off).wait()
        acc = xbuf[which, 0]
        for part in range(1, parts):
            acc = acc + xbuf[which, part]
        return acc

    def halo_copy(side, which, source):
        return pltpu.make_async_remote_copy(
            src_ref=source,
            dst_ref=halo.at[side ^ 1, which],
            send_sem=halo_send.at[side, which],
            recv_sem=halo_recv.at[side ^ 1, which],
            device_id=ids[side],
            device_id_type=MESH,
        )

    def halo_wait(side, which):
        pltpu.make_async_remote_copy(
            src_ref=vals,
            dst_ref=halo.at[side, which],
            send_sem=halo_send.at[side, which],
            recv_sem=halo_recv.at[side, which],
            device_id=ids[side],
            device_id_type=MESH,
        ).wait_recv()

    def far_copy(peer):
        return pltpu.make_async_remote_copy(
            src_ref=far_pack.at[peer],
            dst_ref=far_in.at[col],
            send_sem=far_send.at[peer],
            recv_sem=far_recv.at[col],
            device_id={"wa": peer},
            device_id_type=MESH,
        )

    def far_wait(peer):
        pltpu.make_async_remote_copy(
            src_ref=far_pack.at[peer],
            dst_ref=far_in.at[peer],
            send_sem=far_send.at[peer],
            recv_sem=far_recv.at[peer],
            device_id={"wa": peer},
            device_id_type=MESH,
        ).wait_recv()

    def ret_copy(side):
        return pltpu.make_async_remote_copy(
            src_ref=ret_out.at[side],
            dst_ref=ret_in.at[side ^ 1],
            send_sem=ret_send.at[side],
            recv_sem=ret_recv.at[side ^ 1],
            device_id=ids[side],
            device_id_type=MESH,
        )

    def ret_wait(side):
        pltpu.make_async_remote_copy(
            src_ref=ret_out.at[side],
            dst_ref=ret_in.at[side],
            send_sem=ret_send.at[side],
            recv_sem=ret_recv.at[side],
            device_id=ids[side],
            device_id_type=MESH,
        ).wait_recv()

    def fret_copy(peer):
        return pltpu.make_async_remote_copy(
            src_ref=fret_out.at[peer],
            dst_ref=fret_in.at[col],
            send_sem=fret_send.at[peer],
            recv_sem=fret_recv.at[col],
            device_id={"wa": peer},
            device_id_type=MESH,
        )

    def fret_wait(peer):
        pltpu.make_async_remote_copy(
            src_ref=fret_out.at[peer],
            dst_ref=fret_in.at[peer],
            send_sem=fret_send.at[peer],
            recv_sem=fret_recv.at[peer],
            device_id={"wa": peer},
            device_id_type=MESH,
        ).wait_recv()

    loads[0].wait()
    key_wide = k_raw[...].astype(F32)
    key_squares = row_sums(key_wide * key_wide)
    loads[1].wait()
    query_wide = q_raw[...].astype(F32)
    query_squares = row_sums(query_wide * query_wide)
    sums = lane_columns([(0, query_squares), (1, key_squares)])[0:8]
    loads[2].wait()

    pl.semaphore_wait(
        barrier,
        parts
        - 1
        + jnp.minimum(row, 1)
        + jnp.minimum(rows - 1 - row, 1)
        + (cols - 1),
    )
    x_start(0, sums)
    for side in range(4):

        @pl.when(exists[side])
        def _(side=side):
            halo_copy(side, 1, vals).start()

    loads[3].wait()
    loads[4].wait()
    delta_columns = []
    for head in range(heads):
        lanes = slice(head * hw, (head + 1) * hw)
        product = ups[:, lanes].astype(F32) * outs[:, lanes].astype(F32)
        delta_columns.append((head, jnp.sum(product, axis=1, keepdims=True)))
    delta_ref[...] = lane_columns(delta_columns)[0 : delta_ref.shape[0]]

    mine_used = []
    send_unit = []
    send_used = []
    for peer in range(cols):
        used = jnp.int32(0)
        unit = jnp.int32(0)
        asked = jnp.int32(0)
        for slot in range(slots):
            named = far_ref[0, col, slot] - peer * UNITS
            used = jnp.where((named >= 0) & (named < UNITS), 1, used)
            wanted = far_ref[0, peer, slot] - col * UNITS
            hit = (wanted >= 0) & (wanted < UNITS)
            unit = jnp.where(hit, wanted, unit)
            asked = jnp.where(hit, 1, asked)
        mine_used.append(used)
        send_unit.append(unit)
        send_used.append(asked)

    def pick_unit(peer, source):
        wanted = jnp.full((kb, width), send_unit[peer], jnp.int32)
        picked = source[0:kb, :].astype(F32)
        for unit in range(1, UNITS):
            block = source[unit * kb : (unit + 1) * kb, :].astype(F32)
            picked = jnp.where(wanted == unit, block, picked)
        return picked.astype(BF16)

    for peer in range(cols):

        @pl.when(is_far[peer])
        def _(peer=peer):
            far_pack[peer, 1] = pick_unit(peer, vals)

        @pl.when(jnp.logical_not(is_far[peer]))
        def _(peer=peer):
            far_in[peer] = jnp.zeros(far_in.shape[1:], BF16)

    gain_q = gain_q_ref[...].astype(F32)
    gain_k = gain_k_ref[...].astype(F32)
    rates = lax.rsqrt(x_finish(0) / full_width + EPS)
    rate_columns = to_columns(rates)
    q_rate = rate_columns[:, 0:1]
    k_rate = rate_columns[:, 1:2]
    kn[...] = (k_raw[...].astype(F32) * k_rate * gain_k).astype(BF16)
    for side in range(4):

        @pl.when(exists[side])
        def _(side=side):
            halo_copy(side, 0, kn).start()

    for peer in range(cols):

        @pl.when(is_far[peer])
        def _(peer=peer):
            far_pack[peer, 0] = pick_unit(peer, kn)
            far_copy(peer).start()

    qn[...] = (q_raw[...].astype(F32) * q_rate * gain_q).astype(BF16)

    def attend(head, key_head, value_head, mask):
        lanes = slice(head * hw, (head + 1) * hw)
        query_head = qn[:, lanes]
        upstream_head = ups[:, lanes]
        scores = dot(key_head, query_head, LAST) * score_scale
        weight = jnp.exp(scores - lse_ref[0, 0, head : head + 1, :])
        if mask is not None:
            weight = jnp.where(mask, weight, 0.0)
        dweight = dot(value_head, upstream_head, LAST)
        dscore = (weight * (dweight - delta_ref[head : head + 1, :])).astype(BF16)
        dq_part = dot(dscore, key_head, FIRST)
        dk_part = (dot(dscore, query_head, PLAIN) * score_scale).astype(BF16)
        dv_part = dot(weight.astype(BF16), upstream_head, PLAIN).astype(BF16)
        return dq_part, dk_part, dv_part

    for head in range(heads):
        lanes = slice(head * hw, (head + 1) * hw)
        dq_part, dk_part, dv_part = attend(head, kn[:, lanes], vals[:, lanes], None)
        dq_acc[:, lanes] = dq_part
        total[0, :, lanes] = dk_part.astype(F32)
        total[1, :, lanes] = dv_part.astype(F32)

    for side in range(4):

        @pl.when(exists[side])
        def _(side=side):
            halo_wait(side, 1)
            halo_wait(side, 0)
            for head in range(heads):
                lanes = slice(head * hw, (head + 1) * hw)
                dq_part, dk_part, dv_part = attend(
                    head, halo[side, 0, :, lanes], halo[side, 1, :, lanes], None
                )
                dq_acc[:, lanes] += dq_part
                ret_out[side, 0, :, lanes] = dk_part
                ret_out[side, 1, :, lanes] = dv_part
            ret_copy(side).start()

    for peer in range(cols):

        @pl.when(is_far[peer])
        def _(peer=peer):
            far_wait(peer)

    mask = jnp.concatenate(
        [jnp.full((kb, tokens), used, jnp.int32) for used in mine_used], axis=0
    ) > 0
    for head in range(heads):
        lanes = slice(head * hw, (head + 1) * hw)
        dq_part, dk_part, dv_part = attend(
            head,
            far_in[:, 0, :, lanes].reshape(cols * kb, hw),
            far_in[:, 1, :, lanes].reshape(cols * kb, hw),
            mask,
        )
        dq_acc[:, lanes] += dq_part
        fret_out[:, 0, :, lanes] = dk_part.reshape(cols, kb, hw)
        fret_out[:, 1, :, lanes] = dv_part.reshape(cols, kb, hw)
    for peer in range(cols):

        @pl.when(is_far[peer])
        def _(peer=peer):
            fret_copy(peer).start()

    dq_norm = (dq_acc[...] * score_scale).astype(BF16).astype(F32)
    query_wide = q_raw[...].astype(F32)
    weighted = gain_q * dq_norm
    x_start(1, lane_columns([(0, row_sums(weighted * query_wide))])[0:8])
    q_factor = rates * rates * rates * x_finish(1) / full_width
    q_factor = to_columns(q_factor)[:, 0:1]
    dq_out[0, 0] = (q_rate * weighted - query_wide * q_factor).astype(BF16)

    for side in range(4):

        @pl.when(exists[side])
        def _(side=side):
            ret_wait(side)
            total[...] += ret_in[side].astype(F32)

    for peer in range(cols):

        @pl.when(is_far[peer])
        def _(peer=peer):
            fret_wait(peer)
            for unit in range(UNITS):
                picked = jnp.where(send_unit[peer] == unit, send_used[peer], 0)
                spread = jnp.full((kb, width), picked, jnp.int32) > 0
                place = slice(unit * kb, (unit + 1) * kb)
                for which in range(2):
                    total[which, place, :] += jnp.where(
                        spread, fret_in[peer, which].astype(F32), 0.0
                    )

    dk_norm = total[0].astype(BF16).astype(F32)
    key_wide = k_raw[...].astype(F32)
    weighted = gain_k * dk_norm
    x_start(2, lane_columns([(1, row_sums(weighted * key_wide))])[0:8])
    dv_out[0, 0] = total[1].astype(BF16)
    for side in range(4):

        @pl.when(exists[side])
        def _(side=side):
            halo_copy(side, 1, vals).wait_send()
            halo_copy(side, 0, kn).wait_send()
            ret_copy(side).wait_send()

    for peer in range(cols):

        @pl.when(is_far[peer])
        def _(peer=peer):
            far_copy(peer).wait_send()
            fret_copy(peer).wait_send()

    k_factor = rates * rates * rates * x_finish(2) / full_width
    k_factor = to_columns(k_factor)[:, 1:2]
    dk_out[0, 0] = (k_rate * weighted - key_wide * k_factor).astype(BF16)


def body(sizes, q_raw, k_raw, values, upstream, outputs, logsumexp, gain_q, gain_k, far_list):
    rows, cols, parts = sizes
    tokens, width = q_raw.shape[2:]
    heads = logsumexp.shape[2]
    kb = tokens // UNITS
    delta_rows = -(-heads // 8) * 8
    shape = jax.ShapeDtypeStruct(q_raw.shape, BF16)
    vmem = pl.BlockSpec(memory_space=pltpu.VMEM)
    anywhere = pl.BlockSpec(memory_space=pl.ANY)
    tile = pltpu.VMEM((tokens, width), BF16)
    pair = (2, tokens, width)
    dma = pltpu.SemaphoreType.DMA
    return pl.pallas_call(
        functools.partial(kernel, sizes),
        out_shape=(shape, shape, shape),
        in_specs=[anywhere] * 5 + [vmem] * 3 + [pl.BlockSpec(memory_space=pltpu.SMEM)],
        out_specs=(vmem, vmem, vmem),
        scratch_shapes=[
            tile,
            tile,
            tile,
            tile,
            tile,
            tile,
            tile,
            pltpu.VMEM((delta_rows, tokens), F32),
            pltpu.VMEM((tokens, width), F32),
            pltpu.VMEM((8, 128), F32),
            pltpu.VMEM((4,) + pair, BF16),
            pltpu.VMEM((cols, 2, kb, width), BF16),
            pltpu.VMEM((cols, 2, kb, width), BF16),
            pltpu.VMEM((4,) + pair, BF16),
            pltpu.VMEM((4,) + pair, BF16),
            pltpu.VMEM((cols, 2, kb, width), BF16),
            pltpu.VMEM((cols, 2, kb, width), BF16),
            pltpu.VMEM(pair, F32),
            pltpu.VMEM((3, parts, 8, 128), F32),
            dma((5,)),
            dma((4, 2)),
            dma((4, 2)),
            dma((cols,)),
            dma((cols,)),
            dma((4,)),
            dma((4,)),
            dma((cols,)),
            dma((cols,)),
            dma((3, parts)),
            dma((3, parts)),
        ],
        compiler_params=pltpu.CompilerParams(collective_id=0, has_side_effects=True),
    )(
        q_raw,
        k_raw,
        values,
        upstream,
        outputs,
        logsumexp,
        gain_q.reshape(1, width),
        gain_k.reshape(1, width),
        far_list,
    )


def solution(mesh):
    sizes = (mesh.shape["ha"], mesh.shape["wa"], mesh.shape["hd"])
    tile = P("ha", "wa", None, "hd")
    return jax.shard_map(
        functools.partial(body, sizes),
        mesh=mesh,
        in_specs=(tile,) * 5 + (P("ha", "wa", "hd", None), P("hd"), P("hd"), P("ha", None, None)),
        out_specs=(tile,) * 3,
        check_vma=False,
    )
```

time: 105 us -> 43.2 us (0.41)
  Pallas kernels: 0 us -> 36.4 us
  starting transfers between devices: 30.8 us -> 0 us
  waiting for transfers between devices: 27.1 us -> 0 us
  blocking collectives: 14 us -> 0 us
  other arithmetic: 11.4 us -> 0 us
  matrix products: 8.17 us -> 0 us
  local copies, waits for them, and re-layouts: 11 us -> 5.83 us
    pallas_call x0 -> x1, Pallas kernels: none -> 36.4 us  [body(): pl.pallas_call(functools.partial(kernel, sizes), out_shape=(shape, shape,...]
    ppermute x8 -> x0, waiting for transfers between devices: 27.1 us -> none  [the longest x2 16.5 us: with_halo(): lax.ppermute(tail, axis, [(i, (i + 1) % count) for i in range(ends)])]
    ppermute x8 -> x0, starting transfers between devices: 22.5 us -> none  [the longest x4 11.5 us: shifted(): lax.ppermute(value, axis, [(source, source + steps) for source in range(f...]
    psum x2 -> x0, blocking collectives: 14 us -> none  [the longest x1 8.34 us: body(): lax.psum((jnp.sum(query_wide * query_wide, axis=1), jnp.sum(key_wide * ke...]
    all_to_all x2 -> x0, starting transfers between devices: 8.32 us -> none  [the longest x1 4.87 us: body(): lax.all_to_all(packed, 'wa', split_axis=1, concat_axis=1, tiled=True)]
    dot_general x26 -> x0, matrix products: 8.17 us -> none  [the longest x5 2.64 us: tile_grads(): jnp.dot(dscore, key_head, preferred_element_type=jnp.float32) * score_scale]
    convert_element_type x7 -> x0, other arithmetic: 3.6 us -> none  [the longest x2 1.12 us: body(): key_norm = (key_wide * k_rate[:, None] * gain_kw).astype(jnp.bfloat16)]
    slice x10 -> x0, local copies, waits for them, and re-layouts: 2.56 us -> none  [the longest x2 1.02 us: body(): win_dk = all_dk[:window_len]]
  transfers between devices with their start and end apart: 10 -> 0, of which waited for: 5 -> 0; matrix products, arithmetic and copies ran while one was open for 10% -> 0% of each run, Pallas kernels for 0% -> 0%
where the time goes in v1:
time: 43.2 us; the launch traced here: 42.9 us
  Pallas kernels  36.4 us (84%)
  local copies, waits for them, and re-layouts  5.83 us (13%)
  between operations  0.66 us (2%)
    pallas_call x1, Pallas kernels, body(): pl.pallas_call(functools.partial(kernel, sizes), out_shape=(shape, shape,...  36.4 us
    unnamed x12, local copies, waits for them, and re-layouts  3.98 us
    reshape x1, local copies, waits for them, and re-layouts, body(): gain_q.reshape(1, width)  1.27 us

profile of v1, /device:TPU:0, one launch (start us, length us, event | category | flops | bytes accessed | tf_op | source)
XLA Modules:
  0.0 42.9 jit_solution(1191182873440126894)
XLA Ops:
  0.6 0.0 copy-start.3
  0.6 1.3 %reshape.12.gain_q_ref = bf16[1,640]{1,0:T(2,128)(2,1)} reshape(bf16[640]{0:T(1024)(128)(2,1)} %param.15) | data formatting | bytes 2560 | tf_op jit(solution)/shard_map/reshape | solution.py:496
  1.9 0.0 copy-done.3
  1.9 0.0 copy-start.2
  1.9 0.6 %reshape.13.gain_k_ref = bf16[1,640]{1,0:T(2,128)(2,1)} reshape(bf16[640]{0:T(1024)(128)(2,1)S(1)} %copy-done.3) | data formatting | bytes 2560 | tf_op jit(solution)/shard_map/reshape | solution.py:497
  2.5 0.1 copy-done.2
  2.6 0.6 %copy.12.lse_ref = f32[1,1,5,128]{3,2,1,0:T(8,128)} copy(f32[1,1,5,128]{3,1,2,0:T(1,128)S(1)} %copy-done.2) | data formatting | bytes 5120 | tf_op args[5]
  3.2 36.4 %shard_map.112 = (bf16[1,1,128,640]{3,2,1,0:T(8,128)(2,1)}, bf16[1,1,128,640]{3,2,1,0:T(8,128)(2,1)}, bf16[1,1,128,640]{3,2,1,0:T(8,128)(2,1)}) custom-call(bf16[1,1,128,640]{3,2,1,0:T(8,128)(2,1)} %q_hbm.1, bf16[1,1,128,640]{3,2,1,0:T(8,128)(2,1)} %k_hbm.1, bf16[1,1,128,640]{3,2,1,0:T(8,128)(2,1)} %v_hbm.1, bf16[1,1,128,640]{3,2,1,0:T(8,128)(2,1)} %u_hbm.1, ...), custom_call_target="tpu_custom_call" | custom-call | tf_op jit(solution)/shard_map/pallas_call | solution.py:451
  39.6 0.0 copy-start.1
  39.6 1.6 %copy.16 = bf16[1,1,128,640]{3,2,1,0:T(8,128)(2,1)} copy(bf16[1,1,128,640]{3,2,1,0:T(8,128)(2,1)} %get-tuple-element.6) | data formatting | bytes 327680
  41.2 0.0 copy-done.1
  41.2 0.0 copy-start
  41.2 0.7 %copy.17 = bf16[1,1,128,640]{3,2,1,0:T(8,128)(2,1)} copy(bf16[1,1,128,640]{3,2,1,0:T(8,128)(2,1)S(1)} %copy-done.1) | data formatting | bytes 327680
  41.9 0.3 copy-done
  42.2 0.7 %copy.18 = bf16[1,1,128,640]{3,2,1,0:T(8,128)(2,1)} copy(bf16[1,1,128,640]{3,2,1,0:T(8,128)(2,1)S(1)} %copy-done) | data formatting | bytes 327680
Async XLA Ops:
  0.6 1.3 %copy-start.3 = (bf16[640]{0:T(1024)(128)(2,1)S(1)}, bf16[640]{0:T(1024)(128)(2,1)}, u32[]{:S(2)}) copy-start(bf16[640]{0:T(1024)(128)(2,1)} %param.16) | copy-start | bytes 3844
  1.9 0.7 %copy-start.2 = (f32[1,1,5,128]{3,1,2,0:T(1,128)S(1)}, f32[1,1,5,128]{3,1,2,0:T(1,128)}, u32[]{:S(2)}) copy-start(f32[1,1,5,128]{3,1,2,0:T(1,128)} %param.14) | copy-start | bytes 7684
  39.6 1.6 %copy-start.1 = (bf16[1,1,128,640]{3,2,1,0:T(8,128)(2,1)S(1)}, bf16[1,1,128,640]{3,2,1,0:T(8,128)(2,1)}, u32[]{:S(2)}) copy-start(bf16[1,1,128,640]{3,2,1,0:T(8,128)(2,1)} %get-tuple-element.7) | copy-start | bytes 491524
  41.2 1.0 %copy-start = (bf16[1,1,128,640]{3,2,1,0:T(8,128)(2,1)S(1)}, bf16[1,1,128,640]{3,2,1,0:T(8,128)(2,1)}, u32[]{:S(2)}) copy-start(bf16[1,1,128,640]{3,2,1,0:T(8,128)(2,1)} %get-tuple-element.8) | copy-start | bytes 491524

commit v2 on v1

--- a/solution.py
+++ b/solution.py
@@ -46,7 +46,8 @@
     kn,
     delta_ref,
     dq_acc,
-    own,
+    staged,
+    out_sem,
     halo,
     far_pack,
     far_in,
@@ -73,7 +74,7 @@
     col = lax.axis_index("wa")
     me = lax.axis_index("hd")
     tokens, width = q_raw.shape
-    heads = lse_ref.shape[2]
+    heads = lse_ref.shape[1]
     hw = width // heads
     kb = tokens // UNITS
     full_width = width * parts
@@ -82,12 +83,16 @@
 
     loads = []
     for index, (source, target) in enumerate(
-        ((k_hbm, k_raw), (q_hbm, q_raw), (v_hbm, vals), (u_hbm, ups), (o_hbm, outs))
+        ((v_hbm, vals), (k_hbm, k_raw), (q_hbm, q_raw), (u_hbm, ups), (o_hbm, outs))
     ):
         copy = pltpu.make_async_copy(source.at[0, 0], target, load_sem.at[index])
         copy.start()
         loads.append(copy)
 
+    out_copies = [
+        pltpu.make_async_copy(staged.at[index], target.at[0, 0], out_sem.at[index])
+        for index, target in enumerate((dq_out, dk_out, dv_out))
+    ]
     exists = (row > 0, row < rows - 1, col > 0, col < cols - 1)
     ids = ({"ha": row - 1}, {"ha": row + 1}, {"wa": col - 1}, {"wa": col + 1})
     is_far = [(col - peer) * (col - peer) >= 4 for peer in range(cols)]
@@ -228,14 +233,6 @@
         ).wait_recv()
 
     loads[0].wait()
-    key_wide = k_raw[...].astype(F32)
-    key_squares = row_sums(key_wide * key_wide)
-    loads[1].wait()
-    query_wide = q_raw[...].astype(F32)
-    query_squares = row_sums(query_wide * query_wide)
-    sums = lane_columns([(0, query_squares), (1, key_squares)])[0:8]
-    loads[2].wait()
-
     pl.semaphore_wait(
         barrier,
         parts
@@ -244,12 +241,20 @@
         + jnp.minimum(rows - 1 - row, 1)
         + (cols - 1),
     )
-    x_start(0, sums)
     for side in range(4):
 
         @pl.when(exists[side])
         def _(side=side):
             halo_copy(side, 1, vals).start()
+
+    loads[1].wait()
+    key_wide = k_raw[...].astype(F32)
+    key_squares = row_sums(key_wide * key_wide)
+    loads[2].wait()
+    query_wide = q_raw[...].astype(F32)
+    query_squares = row_sums(query_wide * query_wide)
+    sums = lane_columns([(0, query_squares), (1, key_squares)])[0:8]
+    x_start(0, sums)
 
     loads[3].wait()
     loads[4].wait()
@@ -296,8 +301,8 @@
         def _(peer=peer):
             far_in[peer] = jnp.zeros(far_in.shape[1:], BF16)
 
-    gain_q = gain_q_ref[...].astype(F32)
-    gain_k = gain_k_ref[...].astype(F32)
+    gain_q = gain_q_ref[...].astype(F32).reshape(1, width)
+    gain_k = gain_k_ref[...].astype(F32).reshape(1, width)
     rates = lax.rsqrt(x_finish(0) / full_width + EPS)
     rate_columns = to_columns(rates)
     q_rate = rate_columns[:, 0:1]
@@ -323,7 +328,7 @@
         query_head = qn[:, lanes]
         upstream_head = ups[:, lanes]
         scores = dot(key_head, query_head, LAST) * score_scale
-        weight = jnp.exp(scores - lse_ref[0, 0, head : head + 1, :])
+        weight = jnp.exp(scores - lse_ref[0, head])
         if mask is not None:
             weight = jnp.where(mask, weight, 0.0)
         dweight = dot(value_head, upstream_head, LAST)
@@ -388,7 +393,8 @@
     x_start(1, lane_columns([(0, row_sums(weighted * query_wide))])[0:8])
     q_factor = rates * rates * rates * x_finish(1) / full_width
     q_factor = to_columns(q_factor)[:, 0:1]
-    dq_out[0, 0] = (q_rate * weighted - query_wide * q_factor).astype(BF16)
+    staged[0] = (q_rate * weighted - query_wide * q_factor).astype(BF16)
+    out_copies[0].start()
 
     for side in range(4):
 
@@ -415,7 +421,8 @@
     key_wide = k_raw[...].astype(F32)
     weighted = gain_k * dk_norm
     x_start(2, lane_columns([(1, row_sums(weighted * key_wide))])[0:8])
-    dv_out[0, 0] = total[1].astype(BF16)
+    staged[2] = total[1].astype(BF16)
+    out_copies[2].start()
     for side in range(4):
 
         @pl.when(exists[side])
@@ -433,7 +440,26 @@
 
     k_factor = rates * rates * rates * x_finish(2) / full_width
     k_factor = to_columns(k_factor)[:, 1:2]
-    dk_out[0, 0] = (k_rate * weighted - key_wide * k_factor).astype(BF16)
+    staged[1] = (k_rate * weighted - key_wide * k_factor).astype(BF16)
+    out_copies[1].start()
+    for copy in out_copies:
+        copy.wait()
+
+
+def copy_kernel(dq_in, dk_in, dv_in, dq_out, dk_out, dv_out, stage, in_sem, out_sem):
+    pairs = ((dq_in, dq_out), (dv_in, dv_out), (dk_in, dk_out))
+    into = []
+    back = []
+    for index, (source, target) in enumerate(pairs):
+        into.append(pltpu.make_async_copy(source, stage.at[index], in_sem.at[index]))
+        back.append(pltpu.make_async_copy(stage.at[index], target, out_sem.at[index]))
+    for copy in into:
+        copy.start()
+    for first, second in zip(into, back):
+        first.wait()
+        second.start()
+    for copy in back:
+        copy.wait()
 
 
 def body(sizes, q_raw, k_raw, values, upstream, outputs, logsumexp, gain_q, gain_k, far_list):
@@ -444,15 +470,15 @@
     delta_rows = -(-heads // 8) * 8
     shape = jax.ShapeDtypeStruct(q_raw.shape, BF16)
     vmem = pl.BlockSpec(memory_space=pltpu.VMEM)
-    anywhere = pl.BlockSpec(memory_space=pl.ANY)
+    anywhere = pl.BlockSpec(memory_space=pltpu.HBM)
     tile = pltpu.VMEM((tokens, width), BF16)
     pair = (2, tokens, width)
     dma = pltpu.SemaphoreType.DMA
-    return pl.pallas_call(
+    grads = pl.pallas_call(
         functools.partial(kernel, sizes),
         out_shape=(shape, shape, shape),
         in_specs=[anywhere] * 5 + [vmem] * 3 + [pl.BlockSpec(memory_space=pltpu.SMEM)],
-        out_specs=(vmem, vmem, vmem),
+        out_specs=(anywhere,) * 3,
         scratch_shapes=[
             tile,
             tile,
@@ -463,7 +489,8 @@
             tile,
             pltpu.VMEM((delta_rows, tokens), F32),
             pltpu.VMEM((tokens, width), F32),
-            pltpu.VMEM((8, 128), F32),
+            pltpu.VMEM((3, tokens, width), BF16),
+            dma((3,)),
             pltpu.VMEM((4,) + pair, BF16),
             pltpu.VMEM((cols, 2, kb, width), BF16),
             pltpu.VMEM((cols, 2, kb, width), BF16),
@@ -492,11 +519,18 @@
         values,
         upstream,
         outputs,
-        logsumexp,
-        gain_q.reshape(1, width),
-        gain_k.reshape(1, width),
+        logsumexp.transpose(0, 2, 1, 3),
+        gain_q,
+        gain_k,
         far_list,
     )
+    return pl.pallas_call(
+        copy_kernel,
+        out_shape=(shape, shape, shape),
+        in_specs=[anywhere] * 3,
+        out_specs=(anywhere,) * 3,
+        scratch_shapes=[pltpu.VMEM((3,) + q_raw.shape, BF16), dma((3,)), dma((3,))],
+    )(*grads)
 
 
 def solution(mesh):

time: 43.2 us -> 39 us (0.903)
  local copies, waits for them, and re-layouts: 5.83 us -> 0 us
  Pallas kernels: 36.4 us -> 38.2 us
    unnamed x12 -> x0, local copies, waits for them, and re-layouts: 3.98 us -> none
    reshape x2 -> x0, local copies, waits for them, and re-layouts: 1.85 us -> none  [the longest x1 1.27 us: body(): gain_q.reshape(1, width)]
    pallas_call x0 -> x1, Pallas kernels: none -> 1.79 us  [body(): pl.pallas_call(copy_kernel, out_shape=(shape, shape, shape), in_specs=[an...]
where the time goes in v2:
time: 39 us; the launch traced here: 38.8 us
  Pallas kernels  38.2 us (98%)
  between operations  0.64 us (2%)
    pallas_call x1, Pallas kernels, body(): pl.pallas_call(functools.partial(kernel, sizes), out_shape=(shape, shape,...  36.4 us
    pallas_call x1, Pallas kernels, body(): pl.pallas_call(copy_kernel, out_shape=(shape, shape, shape), in_specs=[an...  1.79 us

profile of v2, /device:TPU:0, one launch (start us, length us, event | category | flops | bytes accessed | tf_op | source)
XLA Modules:
  0.0 38.8 jit_solution(6649524499942061670)
XLA Ops:
  0.6 36.4 %shard_map.112 = (bf16[1,1,128,640]{3,2,1,0:T(8,128)(2,1)}, bf16[1,1,128,640]{3,2,1,0:T(8,128)(2,1)}, bf16[1,1,128,640]{3,2,1,0:T(8,128)(2,1)}) custom-call(bf16[1,1,128,640]{3,2,1,0:T(8,128)(2,1)} %q_hbm.1, bf16[1,1,128,640]{3,2,1,0:T(8,128)(2,1)} %k_hbm.1, bf16[1,1,128,640]{3,2,1,0:T(8,128)(2,1)} %v_hbm.1, bf16[1,1,128,640]{3,2,1,0:T(8,128)(2,1)} %u_hbm.1, ...), custom_call_target="tpu_custom_call" | custom-call | tf_op jit(solution)/shard_map/pallas_call | solution.py:477
  37.0 1.8 %shard_map.113 = (bf16[1,1,128,640]{3,2,1,0:T(8,128)(2,1)}, bf16[1,1,128,640]{3,2,1,0:T(8,128)(2,1)}, bf16[1,1,128,640]{3,2,1,0:T(8,128)(2,1)}) custom-call(bf16[1,1,128,640]{3,2,1,0:T(8,128)(2,1)} %get-tuple-element.6.dq_in, bf16[1,1,128,640]{3,2,1,0:T(8,128)(2,1)} %get-tuple-element.7.dk_in, bf16[1,1,128,640]{3,2,1,0:T(8,128)(2,1)} %get-tuple-element.8.dv_in), custom_call_target="tpu_custom_call" | custom-call | tf_op jit(solution)/shard_map/pallas_call | solution.py:527

commit v3 on v2

--- a/solution.py
+++ b/solution.py
@@ -46,8 +46,6 @@
     kn,
     delta_ref,
     dq_acc,
-    staged,
-    out_sem,
     halo,
     far_pack,
     far_in,
@@ -89,10 +87,6 @@
         copy.start()
         loads.append(copy)
 
-    out_copies = [
-        pltpu.make_async_copy(staged.at[index], target.at[0, 0], out_sem.at[index])
-        for index, target in enumerate((dq_out, dk_out, dv_out))
-    ]
     exists = (row > 0, row < rows - 1, col > 0, col < cols - 1)
     ids = ({"ha": row - 1}, {"ha": row + 1}, {"wa": col - 1}, {"wa": col + 1})
     is_far = [(col - peer) * (col - peer) >= 4 for peer in range(cols)]
@@ -393,8 +387,7 @@
     x_start(1, lane_columns([(0, row_sums(weighted * query_wide))])[0:8])
     q_factor = rates * rates * rates * x_finish(1) / full_width
     q_factor = to_columns(q_factor)[:, 0:1]
-    staged[0] = (q_rate * weighted - query_wide * q_factor).astype(BF16)
-    out_copies[0].start()
+    dq_out[0, 0] = (q_rate * weighted - query_wide * q_factor).astype(BF16)
 
     for side in range(4):
 
@@ -421,8 +414,7 @@
     key_wide = k_raw[...].astype(F32)
     weighted = gain_k * dk_norm
     x_start(2, lane_columns([(1, row_sums(weighted * key_wide))])[0:8])
-    staged[2] = total[1].astype(BF16)
-    out_copies[2].start()
+    dv_out[0, 0] = total[1].astype(BF16)
     for side in range(4):
 
         @pl.when(exists[side])
@@ -440,25 +432,18 @@
 
     k_factor = rates * rates * rates * x_finish(2) / full_width
     k_factor = to_columns(k_factor)[:, 1:2]
-    staged[1] = (k_rate * weighted - key_wide * k_factor).astype(BF16)
-    out_copies[1].start()
-    for copy in out_copies:
-        copy.wait()
-
-
-def copy_kernel(dq_in, dk_in, dv_in, dq_out, dk_out, dv_out, stage, in_sem, out_sem):
-    pairs = ((dq_in, dq_out), (dv_in, dv_out), (dk_in, dk_out))
-    into = []
-    back = []
-    for index, (source, target) in enumerate(pairs):
-        into.append(pltpu.make_async_copy(source, stage.at[index], in_sem.at[index]))
-        back.append(pltpu.make_async_copy(stage.at[index], target, out_sem.at[index]))
-    for copy in into:
+    dk_out[0, 0] = (k_rate * weighted - key_wide * k_factor).astype(BF16)
+
+
+def copy_kernel(dq_in, dk_in, dv_in, dq_out, dk_out, dv_out, sem):
+    pairs = ((dq_in, dq_out), (dk_in, dk_out), (dv_in, dv_out))
+    copies = [
+        pltpu.make_async_copy(source, target, sem.at[index])
+        for index, (source, target) in enumerate(pairs)
+    ]
+    for copy in copies:
         copy.start()
-    for first, second in zip(into, back):
-        first.wait()
-        second.start()
-    for copy in back:
+    for copy in copies:
         copy.wait()
 
 
@@ -476,9 +461,9 @@
     dma = pltpu.SemaphoreType.DMA
     grads = pl.pallas_call(
         functools.partial(kernel, sizes),
-        out_shape=(shape, shape, shape),
+        out_shape=(pltpu.VMEM(q_raw.shape, BF16),) * 3,
         in_specs=[anywhere] * 5 + [vmem] * 3 + [pl.BlockSpec(memory_space=pltpu.SMEM)],
-        out_specs=(anywhere,) * 3,
+        out_specs=(vmem,) * 3,
         scratch_shapes=[
             tile,
             tile,
@@ -489,8 +474,6 @@
             tile,
             pltpu.VMEM((delta_rows, tokens), F32),
             pltpu.VMEM((tokens, width), F32),
-            pltpu.VMEM((3, tokens, width), BF16),
-            dma((3,)),
             pltpu.VMEM((4,) + pair, BF16),
             pltpu.VMEM((cols, 2, kb, width), BF16),
             pltpu.VMEM((cols, 2, kb, width), BF16),
@@ -527,9 +510,10 @@
     return pl.pallas_call(
         copy_kernel,
         out_shape=(shape, shape, shape),
-        in_specs=[anywhere] * 3,
+        in_specs=[vmem] * 3,
         out_specs=(anywhere,) * 3,
-        scratch_shapes=[pltpu.VMEM((3,) + q_raw.shape, BF16), dma((3,)), dma((3,))],
+        scratch_shapes=[dma((3,))],
+        compiler_params=pltpu.CompilerParams(vmem_limit_bytes=4 << 20),
     )(*grads)
 
 

time: 39 us -> 37.3 us (0.956)
  Pallas kernels: 38.2 us -> 36.5 us
    pallas_call x2, Pallas kernels: 38.2 us -> 36.5 us  [the longest x1 35.7 us: body(): pl.pallas_call(functools.partial(kernel, sizes), out_shape=(pltpu.VMEM(q_...]
where the time goes in v3:
time: 37.3 us; the launch traced here: 37.1 us
  Pallas kernels  36.5 us (98%)
  between operations  0.64 us (2%)
    pallas_call x1, Pallas kernels, body(): pl.pallas_call(functools.partial(kernel, sizes), out_shape=(pltpu.VMEM(q_...  35.7 us
    pallas_call x1, Pallas kernels, body(): pl.pallas_call(copy_kernel, out_shape=(shape, shape, shape), in_specs=[vm...  0.8 us

profile of v3, /device:TPU:0, one launch (start us, length us, event | category | flops | bytes accessed | tf_op | source)
XLA Modules:
  0.0 37.1 jit_solution(16036483955361057776)
XLA Ops:
  0.6 35.7 %shard_map.112 = (bf16[1,1,128,640]{3,2,1,0:T(8,128)(2,1)S(1)}, bf16[1,1,128,640]{3,2,1,0:T(8,128)(2,1)S(1)}, bf16[1,1,128,640]{3,2,1,0:T(8,128)(2,1)S(1)}) custom-call(bf16[1,1,128,640]{3,2,1,0:T(8,128)(2,1)} %q_hbm.1, bf16[1,1,128,640]{3,2,1,0:T(8,128)(2,1)} %k_hbm.1, bf16[1,1,128,640]{3,2,1,0:T(8,128)(2,1)} %v_hbm.1, bf16[1,1,128,640]{3,2,1,0:T(8,128)(2,1)} %u_hbm.1, ...), custom_call_target="tpu_custom_call" | custom-call | tf_op jit(solution)/shard_map/pallas_call | solution.py:462
  36.3 0.8 %shard_map.113 = (bf16[1,1,128,640]{3,2,1,0:T(8,128)(2,1)}, bf16[1,1,128,640]{3,2,1,0:T(8,128)(2,1)}, bf16[1,1,128,640]{3,2,1,0:T(8,128)(2,1)}) custom-call(bf16[1,1,128,640]{3,2,1,0:T(8,128)(2,1)S(1)} %get-tuple-element.6.dq_in, bf16[1,1,128,640]{3,2,1,0:T(8,128)(2,1)S(1)} %get-tuple-element.7.dk_in, bf16[1,1,128,640]{3,2,1,0:T(8,128)(2,1)S(1)} %get-tuple-element.8.dv_in), custom_call_target="tpu_custom_call" | custom-call | tf_op jit(solution)/shard_map/pallas_call | solution.py:510

commit v4 on v3

--- a/solution.py
+++ b/solution.py
@@ -166,12 +166,12 @@
             device_id_type=MESH,
         ).wait_recv()
 
-    def far_copy(peer):
+    def far_copy(peer, owner):
         return pltpu.make_async_remote_copy(
             src_ref=far_pack.at[peer],
-            dst_ref=far_in.at[col],
+            dst_ref=far_in.at[owner],
             send_sem=far_send.at[peer],
-            recv_sem=far_recv.at[col],
+            recv_sem=far_recv.at[owner],
             device_id={"wa": peer},
             device_id_type=MESH,
         )
@@ -259,26 +259,26 @@
         delta_columns.append((head, jnp.sum(product, axis=1, keepdims=True)))
     delta_ref[...] = lane_columns(delta_columns)[0 : delta_ref.shape[0]]
 
-    mine_used = []
-    send_unit = []
-    send_used = []
-    for peer in range(cols):
-        used = jnp.int32(0)
+    def unit_of(peer, owner):
         unit = jnp.int32(0)
         asked = jnp.int32(0)
         for slot in range(slots):
-            named = far_ref[0, col, slot] - peer * UNITS
-            used = jnp.where((named >= 0) & (named < UNITS), 1, used)
-            wanted = far_ref[0, peer, slot] - col * UNITS
+            wanted = far_ref[0, peer, slot] - owner * UNITS
             hit = (wanted >= 0) & (wanted < UNITS)
             unit = jnp.where(hit, wanted, unit)
             asked = jnp.where(hit, 1, asked)
-        mine_used.append(used)
-        send_unit.append(unit)
-        send_used.append(asked)
-
-    def pick_unit(peer, source):
-        wanted = jnp.full((kb, width), send_unit[peer], jnp.int32)
+        return unit, asked
+
+    mine_used = [unit_of(col, peer)[1] for peer in range(cols)]
+    send_unit, send_used = zip(*[unit_of(peer, col) for peer in range(cols)])
+    beyond = {
+        LEFT: [(peer > col) & (col > 0) for peer in range(cols)],
+        RIGHT: [(peer < col) & (col < cols - 1) for peer in range(cols)],
+    }
+    owners = {LEFT: col - 1, RIGHT: col + 1}
+
+    def pick_unit(unit_index, source):
+        wanted = jnp.full((kb, width), unit_index, jnp.int32)
         picked = source[0:kb, :].astype(F32)
         for unit in range(1, UNITS):
             block = source[unit * kb : (unit + 1) * kb, :].astype(F32)
@@ -286,10 +286,6 @@
         return picked.astype(BF16)
 
     for peer in range(cols):
-
-        @pl.when(is_far[peer])
-        def _(peer=peer):
-            far_pack[peer, 1] = pick_unit(peer, vals)
 
         @pl.when(jnp.logical_not(is_far[peer]))
         def _(peer=peer):
@@ -307,13 +303,6 @@
         @pl.when(exists[side])
         def _(side=side):
             halo_copy(side, 0, kn).start()
-
-    for peer in range(cols):
-
-        @pl.when(is_far[peer])
-        def _(peer=peer):
-            far_pack[peer, 0] = pick_unit(peer, kn)
-            far_copy(peer).start()
 
     qn[...] = (q_raw[...].astype(F32) * q_rate * gain_q).astype(BF16)
 
@@ -339,12 +328,29 @@
         total[0, :, lanes] = dk_part.astype(F32)
         total[1, :, lanes] = dv_part.astype(F32)
 
-    for side in range(4):
+    for side in (LEFT, RIGHT):
 
         @pl.when(exists[side])
         def _(side=side):
             halo_wait(side, 1)
             halo_wait(side, 0)
+
+        for peer in range(cols):
+
+            @pl.when(beyond[side][peer])
+            def _(side=side, peer=peer):
+                unit = unit_of(peer, owners[side])[0]
+                far_pack[peer, 0] = pick_unit(unit, halo.at[side, 0])
+                far_pack[peer, 1] = pick_unit(unit, halo.at[side, 1])
+                far_copy(peer, owners[side]).start()
+
+    for side in (LEFT, RIGHT, UP, DOWN):
+
+        @pl.when(exists[side])
+        def _(side=side):
+            if side in (UP, DOWN):
+                halo_wait(side, 1)
+                halo_wait(side, 0)
             for head in range(heads):
                 lanes = slice(head * hw, (head + 1) * hw)
                 dq_part, dk_part, dv_part = attend(
@@ -427,8 +433,13 @@
 
         @pl.when(is_far[peer])
         def _(peer=peer):
-            far_copy(peer).wait_send()
             fret_copy(peer).wait_send()
+
+        for side in (LEFT, RIGHT):
+
+            @pl.when(beyond[side][peer])
+            def _(side=side, peer=peer):
+                far_copy(peer, owners[side]).wait_send()
 
     k_factor = rates * rates * rates * x_finish(2) / full_width
     k_factor = to_columns(k_factor)[:, 1:2]

time: 37.3 us -> 37.8 us (1.013)
  Pallas kernels: 36.5 us -> 37 us
    pallas_call x1, Pallas kernels: 35.7 us -> 36.2 us  [body(): pl.pallas_call(functools.partial(kernel, sizes), out_shape=(pltpu.VMEM(q_...]
where the time goes in v4:
time: 37.8 us; the launch traced here: 37.6 us
  Pallas kernels  37 us (98%)
  between operations  0.64 us (2%)
    pallas_call x1, Pallas kernels, body(): pl.pallas_call(functools.partial(kernel, sizes), out_shape=(pltpu.VMEM(q_...  36.2 us
    pallas_call x1, Pallas kernels, body(): pl.pallas_call(copy_kernel, out_shape=(shape, shape, shape), in_specs=[vm...  0.8 us

profile of v4, /device:TPU:0, one launch (start us, length us, event | category | flops | bytes accessed | tf_op | source)
XLA Modules:
  0.0 37.6 jit_solution(14855931692207051576)
XLA Ops:
  0.6 36.2 %shard_map.112 = (bf16[1,1,128,640]{3,2,1,0:T(8,128)(2,1)S(1)}, bf16[1,1,128,640]{3,2,1,0:T(8,128)(2,1)S(1)}, bf16[1,1,128,640]{3,2,1,0:T(8,128)(2,1)S(1)}) custom-call(bf16[1,1,128,640]{3,2,1,0:T(8,128)(2,1)} %q_hbm.1, bf16[1,1,128,640]{3,2,1,0:T(8,128)(2,1)} %k_hbm.1, bf16[1,1,128,640]{3,2,1,0:T(8,128)(2,1)} %v_hbm.1, bf16[1,1,128,640]{3,2,1,0:T(8,128)(2,1)} %u_hbm.1, ...), custom_call_target="tpu_custom_call" | custom-call | tf_op jit(solution)/shard_map/pallas_call | solution.py:473
  36.8 0.8 %shard_map.113 = (bf16[1,1,128,640]{3,2,1,0:T(8,128)(2,1)}, bf16[1,1,128,640]{3,2,1,0:T(8,128)(2,1)}, bf16[1,1,128,640]{3,2,1,0:T(8,128)(2,1)}) custom-call(bf16[1,1,128,640]{3,2,1,0:T(8,128)(2,1)S(1)} %get-tuple-element.6.dq_in, bf16[1,1,128,640]{3,2,1,0:T(8,128)(2,1)S(1)} %get-tuple-element.7.dk_in, bf16[1,1,128,640]{3,2,1,0:T(8,128)(2,1)S(1)} %get-tuple-element.8.dv_in), custom_call_target="tpu_custom_call" | custom-call | tf_op jit(solution)/shard_map/pallas_call | solution.py:521

commit v5 on v3

--- a/solution.py
+++ b/solution.py
@@ -226,7 +226,6 @@
             device_id_type=MESH,
         ).wait_recv()
 
-    loads[0].wait()
     pl.semaphore_wait(
         barrier,
         parts
@@ -239,7 +238,7 @@
 
         @pl.when(exists[side])
         def _(side=side):
-            halo_copy(side, 1, vals).start()
+            halo_copy(side, 1, v_hbm.at[0, 0]).start()
 
     loads[1].wait()
     key_wide = k_raw[...].astype(F32)
@@ -250,6 +249,7 @@
     sums = lane_columns([(0, query_squares), (1, key_squares)])[0:8]
     x_start(0, sums)
 
+    loads[0].wait()
     loads[3].wait()
     loads[4].wait()
     delta_columns = []
@@ -339,7 +339,7 @@
         total[0, :, lanes] = dk_part.astype(F32)
         total[1, :, lanes] = dv_part.astype(F32)
 
-    for side in range(4):
+    for side in (LEFT, RIGHT, UP, DOWN):
 
         @pl.when(exists[side])
         def _(side=side):
@@ -419,7 +419,7 @@
 
         @pl.when(exists[side])
         def _(side=side):
-            halo_copy(side, 1, vals).wait_send()
+            halo_copy(side, 1, v_hbm.at[0, 0]).wait_send()
             halo_copy(side, 0, kn).wait_send()
             ret_copy(side).wait_send()
 

time: 37.3 us -> 37.6 us (level)
  no operation moved by 1% of the time
where the time goes in v5:
time: 37.6 us; the launch traced here: 37.4 us
  Pallas kernels  36.7 us (98%)
  between operations  0.64 us (2%)
    pallas_call x1, Pallas kernels, body(): pl.pallas_call(functools.partial(kernel, sizes), out_shape=(pltpu.VMEM(q_...  35.9 us
    pallas_call x1, Pallas kernels, body(): pl.pallas_call(copy_kernel, out_shape=(shape, shape, shape), in_specs=[vm...  0.8 us

profile of v5, /device:TPU:0, one launch (start us, length us, event | category | flops | bytes accessed | tf_op | source)
XLA Modules:
  0.0 37.4 jit_solution(14608322201658732272)
XLA Ops:
  0.6 35.9 %shard_map.112 = (bf16[1,1,128,640]{3,2,1,0:T(8,128)(2,1)S(1)}, bf16[1,1,128,640]{3,2,1,0:T(8,128)(2,1)S(1)}, bf16[1,1,128,640]{3,2,1,0:T(8,128)(2,1)S(1)}) custom-call(bf16[1,1,128,640]{3,2,1,0:T(8,128)(2,1)} %q_hbm.1, bf16[1,1,128,640]{3,2,1,0:T(8,128)(2,1)} %k_hbm.1, bf16[1,1,128,640]{3,2,1,0:T(8,128)(2,1)} %v_hbm.1, bf16[1,1,128,640]{3,2,1,0:T(8,128)(2,1)} %u_hbm.1, ...), custom_call_target="tpu_custom_call" | custom-call | tf_op jit(solution)/shard_map/pallas_call | solution.py:462
  36.6 0.8 %shard_map.113 = (bf16[1,1,128,640]{3,2,1,0:T(8,128)(2,1)}, bf16[1,1,128,640]{3,2,1,0:T(8,128)(2,1)}, bf16[1,1,128,640]{3,2,1,0:T(8,128)(2,1)}) custom-call(bf16[1,1,128,640]{3,2,1,0:T(8,128)(2,1)S(1)} %get-tuple-element.6.dq_in, bf16[1,1,128,640]{3,2,1,0:T(8,128)(2,1)S(1)} %get-tuple-element.7.dk_in, bf16[1,1,128,640]{3,2,1,0:T(8,128)(2,1)S(1)} %get-tuple-element.8.dv_in), custom_call_target="tpu_custom_call" | custom-call | tf_op jit(solution)/shard_map/pallas_call | solution.py:510
